TPU v7x, 32 devices: a whole 2x2x4 slice. The times are simulated.
32 devices in a mesh: dp: 8 (over z, x), tensor: 4 (over y, core).
Axes of the slice: x: 2, y: 2, z: 4, core: 2. Of those that a mesh axis runs over, the one named last changes fastest.
Arguments:
- inputs: bfloat16 [8192, 4096], P('dp'), may hold values from -6 to 6
- out_grads: bfloat16 [8192, 6144], P('dp', 'tensor'), may hold values from -0.01953125 to 0.01953125
- left_factor: float32 [4096, 4096], P('dp', 'tensor'), may hold values from -6 to 6
- right_factor: float32 [6144, 6144], P('dp', 'tensor'), may hold values from -6 to 6
- left_basis: float32 [4096, 4096], P('dp', 'tensor'), may hold values from -0.09375 to 0.09375
- right_basis: float32 [6144, 6144], P('dp', 'tensor'), may hold values from -0.078125 to 0.078125
Outputs:
- left_new: float32 [4096, 4096], P('dp', 'tensor')
- right_new: float32 [6144, 6144], P('dp', 'tensor')
- rotated: float32 [4096, 6144], P('dp', 'tensor')
All inputs are finite; a program needn't handle non-finite values.
Results may differ from a plain program's by a relative error of at most 0.019.
Values may be sent and summed in bfloat16 or wider, within the bound.
A program may use at most 192 MiB of HBM per device.

v0:
```python
import jax
import jax.numpy as jnp
from jax import lax
from jax.sharding import PartitionSpec as P

F32 = jnp.float32
BF16 = jnp.bfloat16


def mm(a, b, ca, cb):
    return lax.dot_general(a, b, (((ca,), (cb,)), ((), ())), preferred_element_type=F32)


def spread(block, owner, n_dp, n_t):
    me = lax.axis_index("tensor")
    mine = lax.rem(me - owner(lax.axis_index("dp")) + n_t, n_t)
    step = 1
    while step < n_t:
        pairs = []
        for d in range(n_dp):
            for k in range(step):
                if k + step < n_t:
                    src = (owner(d) + k) % n_t
                    dst = (owner(d) + k + step) % n_t
                    pairs.append((d * n_t + src, d * n_t + dst))
        got = lax.ppermute(block, ("dp", "tensor"), pairs)
        block = jnp.where((mine >= step) & (mine < 2 * step), got, block)
        step *= 2
    return block


def shards(inputs, out_grads, left_factor, right_factor, left_basis, right_basis):
    n_dp, n_t = (lax.axis_size("dp"), lax.axis_size("tensor"))
    krows, kcols = left_factor.shape
    mrows, mcols = right_factor.shape
    dp = lax.axis_index("dp")
    left_low = left_basis.astype(BF16)
    left_rows = lax.all_gather(left_low, "tensor", axis=1, tiled=True)
    left_cols = lax.all_to_all(left_rows, "dp", split_axis=1, concat_axis=0, tiled=True)
    basis_panel = lax.all_gather(right_basis.astype(BF16), "dp", axis=0, tiled=True)
    summed = lax.psum_scatter(
        mm(inputs, out_grads, 0, 0).astype(BF16), "dp", scatter_dimension=0, tiled=True
    )
    col_panel = lax.all_gather(summed, "dp", axis=0, tiled=True)
    turned = mm(left_cols, col_panel, 0, 0).astype(BF16)
    turned_rows = lax.all_gather(turned, "tensor", axis=1, tiled=True)
    own = lax.dynamic_slice_in_dim(col_panel, lax.rem(dp * mrows, mcols), mrows, 1)
    own = spread(own, lambda d: d * mrows // mcols, n_dp, n_t)
    parts = jnp.einsum(
        "jkc,rc->jrk", col_panel.reshape(n_t, kcols, mcols), summed, preferred_element_type=F32
    ).astype(BF16)
    gram_left = lax.psum_scatter(
        parts.reshape(n_t * krows, kcols), "tensor", scatter_dimension=0, tiled=True
    ).astype(F32)
    left_new = 0.95 * left_factor + 0.05 * gram_left
    right_new = 0.95 * right_factor + 0.05 * mm(own, col_panel, 0, 0)
    rotated = mm(turned_rows, basis_panel, 1, 0)
    return (left_new, right_new, rotated)


def solution(mesh):
    spec = P("dp", "tensor")
    return jax.shard_map(
        shards,
        mesh=mesh,
        in_specs=(P("dp", None), spec, spec, spec, spec, spec),
        out_specs=(spec, spec, spec),
        check_vma=False,
    )
```

profile of v0, /device:TPU:0, one launch (start us, length us, event | category | flops | bytes accessed | tf_op | source)
XLA Modules:
  0.0 975.2 jit_solution(8591873962908227927)
XLA Ops:
  7.2 0.0 copy-start
  7.2 0.0 reduce-scatter.3.cloned.1.call-start
  7.2 1.8 copy-done
  9.1 19.1 %convolution_convert_fusion = bf16[4096,1536]{1,0:T(8,128)(2,1)} fusion(bf16[1024,4096]{1,0:T(8,128)(2,1)} %param.6, bf16[1024,1536]{1,0:T(8,128)(2,1)S(1)} %copy-done), kind=kOutput, calls=%fused_computation | convolution fusion | flops 12891193344 | bytes 24117248 | tf_op jit(solution)/shard_map/dot_general | solution.py:11
  28.2 0.0 copy-start.2
  28.2 0.0 reduce-scatter.3.cloned.1.call-update
  28.2 0.0 all-gather.5.cloned.1.call-start
  28.3 210.1 %reduce-scatter.3.cloned.1.call-done = bf16[512,1536]{1,0:T(8,128)(2,1)} async-done(((bf16[4096,1536]{1,0:T(8,128)(2,1)}), bf16[512,1536]{1,0:T(8,128)(2,1)}) %reduce-scatter.3.cloned.1.call-update) | async-done | bytes 1572880 | tf_op jit(solution)/shard_map/reduce_scatter | solution.py:41
  238.4 0.0 all-gather.5.cloned.1.call-update
  238.4 0.0 all-gather.7.cloned.1.call-start
  238.4 0.0 copy-done.2
  238.4 1.4 copy.9
  239.8 0.0 all-gather.7.cloned.1.call-update
  239.8 0.0 reduce-scatter.5.cloned.1.call-start
  239.9 176.2 %all-gather.5.cloned.1.call-done = bf16[4096,1536]{1,0:T(8,128)(2,1)} async-done(((bf16[512,1536]{1,0:T(8,128)(2,1)}), bf16[4096,1536]{1,0:T(8,128)(2,1)}) %all-gather.5.cloned.1.call-update) | async-done | bytes 12582928 | tf_op jit(solution)/shard_map/all_gather | solution.py:44
  416.1 11.4 %convolution_convert_fusion.2 = bf16[512,4,1024]{2,0,1:T(8,128)(2,1)} fusion(bf16[4,1024,1536]{2,1,0:T(8,128)(2,1)} %bitcast.20, bf16[512,1536]{1,0:T(8,128)(2,1)} %reduce-scatter.3.cloned.1.call-done), kind=kOutput, calls=%fused_computation.8 | convolution fusion | flops 6444548096 | bytes 18350080 | tf_op jit(solution)/shard_map/jkc,rc->jrk/dot_general | solution.py:49
  427.5 0.0 reduce-scatter.5.cloned.1.call-update
  427.6 0.0 all-gather.11.cloned.1.call-start
  427.6 4.0 convert_element_type.31
  431.6 0.0 all-gather.11.cloned.1.call-update
  431.7 19.3 %all-gather.7.cloned.1.call-done = bf16[512,4096]{0,1:T(8,128)(2,1)} async-done(((bf16[512,1024]{0,1:T(8,128)(2,1)}), bf16[512,4096]{0,1:T(8,128)(2,1)}) %all-gather.7.cloned.1.call-update) | async-done | bytes 4194320 | tf_op jit(solution)/shard_map/all_gather | solution.py:38
  450.9 5.5 all-to-all-start
  456.4 0.0 all-gather.9.cloned.1.call-start
  456.5 9.8 %constant_dynamic-slice_fusion = bf16[4096,768]{1,0:T(8,128)(2,1)} fusion(bf16[4096,1536]{1,0:T(8,128)(2,1)} %all-gather.5.cloned.1.call-done, s32[]{:T(128)S(6)} %select_n.25), kind=kLoop, calls=%fused_computation.11 | loop fusion | bytes 12582916 | tf_op jit(solution)/shard_map/dynamic_slice | solution.py:47
  466.3 4.3 collective-permute-start
  470.6 101.8 %all-to-all-done = bf16[512,8,512]{0,2,1:T(8,128)(2,1)} async-done(((bf16[512,8,512]{0,2,1:T(8,128)(2,1)}), bf16[512,8,512]{0,2,1:T(8,128)(2,1)}, u32[]{:S(2)}, u32[]{:S(2)}) %all-to-all-start) | async-done | bytes 4194336 | tf_op jit(solution)/shard_map/all_to_all | solution.py:39
  572.4 6.5 copy.10
  578.9 11.9 %fusion.5 = bf16[512,1536]{0,1:T(8,128)(2,1)} fusion(bf16[4096,1536]{1,0:T(8,128)(2,1)} %all-gather.5.cloned.1.call-done, bf16[4096,512]{1,0:T(8,128)(2,1)} %bitcast.23), kind=kOutput, calls=%fused_computation.7 | convolution fusion | flops 6443237376 | bytes 18350080 | tf_op jit(solution)/shard_map/dot_general | solution.py:11
  590.8 0.0 all-gather.9.cloned.1.call-update
  590.8 0.0 copy-start.3
  590.9 0.0 collective-permute-done
  590.9 10.3 %broadcast_select_fusion = bf16[4096,768]{1,0:T(8,128)(2,1)} fusion(bf16[4096,768]{1,0:T(8,128)(2,1)} %collective-permute-done, pred[]{:T(512)S(6)} %and.15, bf16[4096,1536]{1,0:T(8,128)(2,1)} %all-gather.5.cloned.1.call-done, s32[]{:T(128)S(6)} %select_n.25), kind=kLoop, calls=%fused_computation.3 | loop fusion | flops 3145728 | bytes 18874372 | tf_op jit(solution)/shard_map/jit(_where)/select_n | solution.py:27
  601.1 5.2 collective-permute-start.1
  606.4 0.0 reduce-scatter.5.cloned.1.call-done
  606.4 0.0 copy-done.3
  606.4 3.0 multiply_add_fusion.1
  609.4 274.1 %all-gather.11.cloned.1.call-done = bf16[6144,1536]{1,0:T(8,128)(2,1)} async-done(((bf16[768,1536]{1,0:T(8,128)(2,1)}), bf16[6144,1536]{1,0:T(8,128)(2,1)}) %all-gather.11.cloned.1.call-update) | async-done | bytes 18874384 | tf_op jit(solution)/shard_map/all_gather | solution.py:40
  883.6 49.6 %all-gather.9.cloned.1.call-done = bf16[512,6144]{0,1:T(8,128)(2,1)} async-done(((bf16[512,1536]{0,1:T(8,128)(2,1)}), bf16[512,6144]{0,1:T(8,128)(2,1)}) %all-gather.9.cloned.1.call-update) | async-done | bytes 6291472 | tf_op jit(solution)/shard_map/all_gather | solution.py:46
  933.2 16.9 %fusion.7 = f32[512,1536]{1,0:T(8,128)} fusion(bf16[512,6144]{0,1:T(8,128)(2,1)} %all-gather.9.cloned.1.call-done, bf16[6144,1536]{1,0:T(8,128)(2,1)} %all-gather.11.cloned.1.call-done), kind=kOutput, calls=%fused_computation.12 | convolution fusion | flops 9663676416 | bytes 28311552 | tf_op jit(solution)/shard_map/dot_general | solution.py:11
  950.1 0.0 collective-permute-done.1
  950.1 0.0 copy-start.1
  950.1 18.2 %multiply_add_fusion = f32[768,1536]{1,0:T(8,128)} fusion(f32[768,1536]{1,0:T(8,128)} %param.9, bf16[4096,1536]{1,0:T(8,128)(2,1)} %all-gather.5.cloned.1.call-done, bf16[4096,768]{1,0:T(8,128)(2,1)} %collective-permute-done.1, bf16[4096,768]{1,0:T(8,128)(2,1)} %broadcast_select_fusion, pred[]{:T(512)S(6)} %and.14), kind=kOutput, calls=%fused_computation.5 | convolution fusion | flops 9670361088 | bytes 34603008 | tf_op jit(solution)/shard_map/dot_general | solution.py:11
  968.3 0.0 copy-done.1
Async XLA Ops:
  7.2 1.9 copy-start
  7.2 231.2 %reduce-scatter.3.cloned.1.call-start = ((), (), s32[]{:S(2)}) async-start(), calls=%async_computation.3 | async-start | bytes 14155776 | tf_op jit(solution)/shard_map/reduce_scatter | solution.py:41
  28.2 210.2 %copy-start.2 = (f32[512,1024]{1,0:T(8,128)S(1)}, f32[512,1024]{1,0:T(8,128)}, u32[]{:S(2)}) copy-start(f32[512,1024]{1,0:T(8,128)} %param.10) | copy-start | bytes 6291460
  28.2 387.9 %all-gather.5.cloned.1.call-start = ((), (), s32[]{:S(2)}) async-start(), calls=%async_computation.4 | async-start | bytes 14155776 | tf_op jit(solution)/shard_map/all_gather | solution.py:44
  238.4 212.6 %all-gather.7.cloned.1.call-start = ((), (), s32[]{:S(2)}) async-start(), calls=%async_computation.6 | async-start | bytes 5242880 | tf_op jit(solution)/shard_map/all_gather | solution.py:38
  239.8 366.6 %reduce-scatter.5.cloned.1.call-start = ((), (), s32[]{:S(2)}) async-start(), calls=%async_computation.5 | async-start | bytes 5242880 | tf_op jit(solution)/shard_map/reduce_scatter | solution.py:52
  427.6 456.0 %all-gather.11.cloned.1.call-start = ((), (), s32[]{:S(2)}) async-start(), calls=%async_computation.8 | async-start | bytes 21233664 | tf_op jit(solution)/shard_map/all_gather | solution.py:40
  450.9 121.4 %all-to-all-start = ((bf16[512,8,512]{0,2,1:T(8,128)(2,1)}), bf16[512,8,512]{0,2,1:T(8,128)(2,1)}, u32[]{:S(2)}, u32[]{:S(2)}) async-start(bf16[512,8,512]{0,2,1:T(8,128)(2,1)} %bitcast.22), calls=%async_computation.2 | async-start | bytes 8388608 | tf_op jit(solution)/shard_map/all_to_all | solution.py:39
  456.4 476.8 %all-gather.9.cloned.1.call-start = ((), (), s32[]{:S(2)}) async-start(), calls=%async_computation.7 | async-start | bytes 7864320 | tf_op jit(solution)/shard_map/all_gather | solution.py:46
  466.3 124.5 %collective-permute-start = (bf16[4096,768]{1,0:T(8,128)(2,1)}, bf16[4096,768]{1,0:T(8,128)(2,1)}, u32[]{:S(2)}, u32[]{:S(2)}) collective-permute-start(bf16[4096,768]{1,0:T(8,128)(2,1)} %constant_dynamic-slice_fusion), channel_id=1, source_target_pairs={{0,1},{4,5},{9,10},{13,14},{18,19},{22,23},{27,24},{31,28}} | collective-permute-start | bytes 18874376 | tf_op jit(solution)/shard_map/ppermute | solution.py:26
  590.8 15.6 %copy-start.3 = (f32[512,1024]{1,0:T(8,128)S(1)}, f32[512,1024]{1,0:T(8,128)}, u32[]{:S(2)}) copy-start(f32[512,1024]{1,0:T(8,128)} %param.8) | copy-start | bytes 6291460
  601.1 349.0 %collective-permute-start.1 = (bf16[4096,768]{1,0:T(8,128)(2,1)}, bf16[4096,768]{1,0:T(8,128)(2,1)}, u32[]{:S(2)}, u32[]{:S(2)}) collective-permute-start(bf16[4096,768]{1,0:T(8,128)(2,1)} %broadcast_select_fusion), channel_id=1, source_target_pairs={{0,2},{1,3},{4,6},{5,7},{9,11},{10,8},{13,15},{14,12},{18,16},{19,... | collective-permute-start | bytes 18874376 | tf_op jit(solution)/shard_map/ppermute | solution.py:26
  950.1 18.2 %copy-start.1 = (bf16[1024,1536]{1,0:T(8,128)(2,1)S(1)}, bf16[1024,1536]{1,0:T(8,128)(2,1)}, u32[]{:S(2)}) copy-start(bf16[1024,1536]{1,0:T(8,128)(2,1)} %param.7) | copy-start | bytes 9437188
Sparse Core Ops, SparseCore 0:
  28.4 209.9 reduce-scatter.2
  240.6 175.4 all-gather.4
  418.2 32.6 all-gather.6
  453.9 44.5 reduce-scatter.4
  500.5 383.0 all-gather.10
  885.1 48.1 all-gather.8
where the time goes:
time: 976 us; the launch traced here: 975 us
  waiting for transfers between devices  831 us (85%)
  matrix products  77.6 us (8%)
  local copies, waits for them, and re-layouts  19.6 us (2%)
  other arithmetic  17.4 us (2%)
  starting transfers between devices  15.3 us (2%)
  between operations  14.2 us (1%)
    all_gather x1, waiting for transfers between devices, shards(): lax.all_gather(right_basis.astype(BF16), 'dp', axis=0, tiled=True)  274 us
    reduce_scatter x1, waiting for transfers between devices, shards(): lax.psum_scatter(mm(inputs, out_grads, 0, 0).astype(BF16), 'dp', scatter_...  210 us
    all_gather x1, waiting for transfers between devices, shards(): col_panel = lax.all_gather(summed, 'dp', axis=0, tiled=True)  176 us
    all_to_all x1, waiting for transfers between devices, shards(): lax.all_to_all(left_rows, 'dp', split_axis=1, concat_axis=0, tiled=True)  102 us
    dot_general x4, matrix products, mm(): lax.dot_general(a, b, (((ca,), (cb,)), ((), ())), preferred_element_type=...  66.1 us
    all_gather x1, waiting for transfers between devices, shards(): turned_rows = lax.all_gather(turned, 'tensor', axis=1, tiled=True)  49.6 us
  transfers between devices with their start and end apart: 9, of which 6 were waited for; matrix products, arithmetic and copies ran while one was open for 8% of the time, Pallas kernels for 0%

commit v1 on v0

--- a/solution.py
+++ b/solution.py
@@ -37,7 +37,24 @@
     left_low = left_basis.astype(BF16)
     left_rows = lax.all_gather(left_low, "tensor", axis=1, tiled=True)
     left_cols = lax.all_to_all(left_rows, "dp", split_axis=1, concat_axis=0, tiled=True)
-    basis_panel = lax.all_gather(right_basis.astype(BF16), "dp", axis=0, tiled=True)
+    value = right_basis.astype(BF16)
+    size, index, span = (lax.axis_size("dp"), lax.axis_index("dp"), value.shape[0])
+    forward = [(i, (i + 1) % size) for i in range(size)]
+    left = [(i, (i - 1) % size) for i in range(size)]
+    basis_panel = jnp.zeros((*value.shape[:0], size * span, *value.shape[0 + 1 :]), value.dtype)
+    basis_panel = lax.dynamic_update_slice_in_dim(basis_panel, value, index * span, axis=0)
+    from_left = from_right = value
+    halfway = size // 2
+    for step_2 in range(1, halfway + 1):
+        from_left = lax.ppermute(from_left, "dp", forward)
+        basis_panel = lax.dynamic_update_slice_in_dim(
+            basis_panel, from_left, (index - step_2) % size * span, axis=0
+        )
+        if step_2 < size - halfway:
+            from_right = lax.ppermute(from_right, "dp", left)
+            basis_panel = lax.dynamic_update_slice_in_dim(
+                basis_panel, from_right, (index + step_2) % size * span, axis=0
+            )
     summed = lax.psum_scatter(
         mm(inputs, out_grads, 0, 0).astype(BF16), "dp", scatter_dimension=0, tiled=True
     )

time: 976 us -> 945 us (0.968)
  waiting for transfers between devices: 831 us -> 745 us
  local copies, waits for them, and re-layouts: 19.6 us -> 48.9 us
  starting transfers between devices: 15.3 us -> 34.2 us
    ppermute x0 -> x7, waiting for transfers between devices: none -> 291 us  [the longest x4 291 us: shards(): from_left = lax.ppermute(from_left, 'dp', forward)]
    all_gather x1 -> x0, waiting for transfers between devices: 274 us -> none  [shards(): lax.all_gather(right_basis.astype(BF16), 'dp', axis=0, tiled=True)]
    all_to_all x1, waiting for transfers between devices: 102 us -> 0.01 us  [shards(): lax.all_to_all(left_rows, 'dp', split_axis=1, concat_axis=0, tiled=True)]
    all_gather x1, waiting for transfers between devices: 176 us -> 246 us  [shards(): col_panel = lax.all_gather(summed, 'dp', axis=0, tiled=True)]
    all_gather x1, waiting for transfers between devices: 49.6 us -> 0.01 us  [shards(): turned_rows = lax.all_gather(turned, 'tensor', axis=1, tiled=True)]
    dynamic_update_slice x0 -> x7, local copies, waits for them, and re-layouts: none -> 21.2 us  [the longest x4 11.4 us: shards(): lax.dynamic_update_slice_in_dim(basis_panel, from_left, (index - step_2)...]
    all_gather x1, waiting for transfers between devices: 19.3 us -> 0.02 us  [shards(): left_rows = lax.all_gather(left_low, 'tensor', axis=1, tiled=True)]
    ppermute x0 -> x7, starting transfers between devices: none -> 16.4 us  [the longest x4 8.96 us: shards(): from_left = lax.ppermute(from_left, 'dp', forward)]
  transfers between devices with their start and end apart: 9 -> 15, of which waited for: 6 -> 6; matrix products, arithmetic and copies ran while one was open for 8% -> 11% of each run, Pallas kernels for 0% -> 0%
where the time goes in v1:
time: 945 us; the launch traced here: 944 us
  waiting for transfers between devices  745 us (79%)
  matrix products  84.4 us (9%)
  local copies, waits for them, and re-layouts  48.9 us (5%)
  starting transfers between devices  34.2 us (4%)
  other arithmetic  15.8 us (2%)
  between operations  15.8 us (2%)
    ppermute x4, waiting for transfers between devices, shards(): from_left = lax.ppermute(from_left, 'dp', forward)  291 us
    all_gather x1, waiting for transfers between devices, shards(): col_panel = lax.all_gather(summed, 'dp', axis=0, tiled=True)  246 us
    reduce_scatter x1, waiting for transfers between devices, shards(): lax.psum_scatter(mm(inputs, out_grads, 0, 0).astype(BF16), 'dp', scatter_...  207 us
    dot_general x4, matrix products, mm(): lax.dot_general(a, b, (((ca,), (cb,)), ((), ())), preferred_element_type=...  66.2 us
  transfers between devices with their start and end apart: 15, of which 6 were waited for; matrix products, arithmetic and copies ran while one was open for 11% of the time, Pallas kernels for 0%

profile of v1, /device:TPU:0, one launch (start us, length us, event | category | flops | bytes accessed | tf_op | source)
XLA Modules:
  0.0 943.6 jit_solution(3420228233270420374)
XLA Ops:
  8.0 0.0 reduce-scatter.3.cloned.1.call-start
  8.1 1.8 copy-done
  9.9 19.2 %convolution_convert_fusion = bf16[4096,1536]{1,0:T(8,128)(2,1)} fusion(bf16[1024,4096]{1,0:T(8,128)(2,1)} %param.6, bf16[1024,1536]{1,0:T(8,128)(2,1)S(1)} %copy-done), kind=kOutput, calls=%fused_computation | convolution fusion | flops 12891193344 | bytes 24117248 | tf_op jit(solution)/shard_map/dot_general | solution.py:11
  29.1 0.0 reduce-scatter.3.cloned.1.call-update
  29.1 0.0 all-gather.6.cloned.1.call-start
  29.1 1.5 copy-done.2
  30.6 1.4 copy.9
  32.0 0.0 all-gather.6.cloned.1.call-update
  32.0 0.0 all-gather.4.cloned.1.call-start
  32.1 207.1 %reduce-scatter.3.cloned.1.call-done = bf16[512,1536]{1,0:T(8,128)(2,1)} async-done(((bf16[4096,1536]{1,0:T(8,128)(2,1)}), bf16[512,1536]{1,0:T(8,128)(2,1)}) %reduce-scatter.3.cloned.1.call-update) | async-done | bytes 1572880 | tf_op jit(solution)/shard_map/reduce_scatter | solution.py:58
  239.2 0.0 all-gather.4.cloned.1.call-update
  239.2 0.0 all-gather.6.cloned.1.call-done
  239.3 4.7 all-to-all-start
  244.0 0.0 reduce-scatter.5.cloned.1.call-start
  244.0 246.0 %all-gather.4.cloned.1.call-done = bf16[4096,1536]{1,0:T(8,128)(2,1)} async-done(((bf16[512,1536]{1,0:T(8,128)(2,1)}), bf16[4096,1536]{1,0:T(8,128)(2,1)}) %all-gather.4.cloned.1.call-update) | async-done | bytes 12582928 | tf_op jit(solution)/shard_map/all_gather | solution.py:61
  490.0 18.3 %convolution_convert_fusion.2 = bf16[512,4,1024]{2,0,1:T(8,128)(2,1)} fusion(bf16[4,1024,1536]{2,1,0:T(8,128)(2,1)} %bitcast.20, bf16[512,1536]{1,0:T(8,128)(2,1)S(1)} %copy-done.4), kind=kOutput, calls=%fused_computation.8 | convolution fusion | flops 6444548096 | bytes 18350080 | tf_op jit(solution)/shard_map/jkc,rc->jrk/dot_general | solution.py:66
  508.3 0.0 reduce-scatter.5.cloned.1.call-update
  508.3 0.0 all-gather.8.cloned.1.call-start
  508.4 9.8 %constant_dynamic-slice_fusion = bf16[4096,768]{1,0:T(8,128)(2,1)} fusion(bf16[4096,1536]{1,0:T(8,128)(2,1)} %all-gather.4.cloned.1.call-done, s32[]{:T(128)S(6)} %select_n.79), kind=kLoop, calls=%fused_computation.19 | loop fusion | bytes 12582916 | tf_op jit(solution)/shard_map/dynamic_slice | solution.py:64
  518.2 4.8 collective-permute-start
  523.1 6.7 broadcast_in_dim.3
  529.7 2.6 constant_dynamic-update-slice_fusion.7
  532.3 1.5 collective-permute-start.2
  533.8 6.4 copy.10
  540.2 11.8 %fusion.5 = bf16[512,1536]{0,1:T(8,128)(2,1)} fusion(bf16[4096,1536]{1,0:T(8,128)(2,1)} %all-gather.4.cloned.1.call-done, bf16[4096,512]{1,0:T(8,128)(2,1)} %bitcast.25), kind=kOutput, calls=%fused_computation.7 | convolution fusion | flops 6443237376 | bytes 18350080 | tf_op jit(solution)/shard_map/dot_general | solution.py:11
  552.1 0.0 all-gather.8.cloned.1.call-update
  552.1 3.2 collective-permute-start.3
  555.3 78.3 %collective-permute-done.2 = bf16[768,1536]{1,0:T(8,128)(2,1)S(1)} collective-permute-done((bf16[768,1536]{1,0:T(8,128)(2,1)}, bf16[768,1536]{1,0:T(8,128)(2,1)S(1)}, u32[]{:S(2)}, u32[]{:S(2)}) %collective-permute-start.2) | collective-permute-done | bytes 2359328 | tf_op jit(solution)/shard_map/ppermute | solution.py:49
  633.6 2.4 collective-permute-start.4
  636.0 2.3 collective-permute-start.5
  638.3 96.7 %collective-permute-done.4 = bf16[768,1536]{1,0:T(8,128)(2,1)} collective-permute-done((bf16[768,1536]{1,0:T(8,128)(2,1)S(1)}, bf16[768,1536]{1,0:T(8,128)(2,1)}, u32[]{:S(2)}, u32[]{:S(2)}) %collective-permute-start.4) | collective-permute-done | bytes 2359328 | tf_op jit(solution)/shard_map/ppermute | solution.py:49
  735.1 2.6 collective-permute-start.6
  737.7 10.2 %broadcast_select_fusion = bf16[4096,768]{1,0:T(8,128)(2,1)} fusion(bf16[4096,768]{1,0:T(8,128)(2,1)} %collective-permute-done, pred[]{:T(512)S(6)} %and.44, bf16[4096,1536]{1,0:T(8,128)(2,1)} %all-gather.4.cloned.1.call-done, s32[]{:T(128)S(6)} %select_n.79), kind=kLoop, calls=%fused_computation.3 | loop fusion | flops 3145728 | bytes 18874372 | tf_op jit(solution)/shard_map/jit(_where)/select_n | solution.py:27
  747.8 8.0 collective-permute-start.1
  755.9 1.9 collective-permute-start.7
  757.7 79.4 %collective-permute-done.6 = bf16[768,1536]{1,0:T(8,128)(2,1)} collective-permute-done((bf16[768,1536]{1,0:T(8,128)(2,1)}, bf16[768,1536]{1,0:T(8,128)(2,1)}, u32[]{:S(2)}, u32[]{:S(2)}) %collective-permute-start.6) | collective-permute-done | bytes 2359328 | tf_op jit(solution)/shard_map/ppermute | solution.py:49
  837.1 2.5 collective-permute-start.8
  839.6 1.6 constant_dynamic-update-slice_fusion.6
  841.2 3.3 constant_dynamic-update-slice_fusion.5
  844.5 3.2 constant_dynamic-update-slice_fusion.4
  847.7 3.3 constant_dynamic-update-slice_fusion.3
  851.0 3.4 constant_dynamic-update-slice_fusion.2
  854.4 3.3 constant_dynamic-update-slice_fusion.1
  857.7 36.8 %collective-permute-done.8 = bf16[768,1536]{1,0:T(8,128)(2,1)} collective-permute-done((bf16[768,1536]{1,0:T(8,128)(2,1)}, bf16[768,1536]{1,0:T(8,128)(2,1)}, u32[]{:S(2)}, u32[]{:S(2)}) %collective-permute-start.8) | collective-permute-done | bytes 2359328 | tf_op jit(solution)/shard_map/ppermute | solution.py:49
  894.5 3.2 constant_dynamic-update-slice_fusion
  897.7 3.0 multiply_add_fusion.1
  900.8 17.0 %fusion.7 = f32[512,1536]{1,0:T(8,128)} fusion(bf16[512,6144]{0,1:T(8,128)(2,1)} %all-gather.8.cloned.1.call-done, bf16[6144,1536]{1,0:T(8,128)(2,1)} %constant_dynamic-update-slice_fusion), kind=kOutput, calls=%fused_computation.20 | convolution fusion | flops 9663676416 | bytes 28311552 | tf_op jit(solution)/shard_map/dot_general | solution.py:11
  917.8 18.2 %multiply_add_fusion = f32[768,1536]{1,0:T(8,128)} fusion(f32[768,1536]{1,0:T(8,128)} %param.9, bf16[4096,1536]{1,0:T(8,128)(2,1)} %all-gather.4.cloned.1.call-done, bf16[4096,768]{1,0:T(8,128)(2,1)} %collective-permute-done.1, bf16[4096,768]{1,0:T(8,128)(2,1)} %broadcast_select_fusion, pred[]{:T(512)S(6)} %and.43), kind=kOutput, calls=%fused_computation.5 | convolution fusion | flops 9670361088 | bytes 34603008 | tf_op jit(solution)/shard_map/dot_general | solution.py:11
  (21 shorter events, 0.1 us)
Async XLA Ops:
  8.0 1.9 copy-start
  8.0 231.2 %reduce-scatter.3.cloned.1.call-start = ((), (), s32[]{:S(2)}) async-start(), calls=%async_computation.3 | async-start | bytes 14155776 | tf_op jit(solution)/shard_map/reduce_scatter | solution.py:58
  29.1 1.6 copy-start.2
  29.1 210.2 %all-gather.6.cloned.1.call-start = ((), (), s32[]{:S(2)}) async-start(), calls=%async_computation.6 | async-start | bytes 5242880 | tf_op jit(solution)/shard_map/all_gather | solution.py:38
  32.0 458.0 %all-gather.4.cloned.1.call-start = ((), (), s32[]{:S(2)}) async-start(), calls=%async_computation.4 | async-start | bytes 14155776 | tf_op jit(solution)/shard_map/all_gather | solution.py:61
  239.2 250.8 %copy-start.4 = (bf16[512,1536]{1,0:T(8,128)(2,1)S(1)}, bf16[512,1536]{1,0:T(8,128)(2,1)}, u32[]{:S(2)}) copy-start(bf16[512,1536]{1,0:T(8,128)(2,1)} %reduce-scatter.3.cloned.1.call-done) | copy-start | bytes 4718596
  239.3 294.6 %all-to-all-start = ((bf16[512,8,512]{0,2,1:T(8,128)(2,1)}), bf16[512,8,512]{0,2,1:T(8,128)(2,1)}, u32[]{:S(2)}, u32[]{:S(2)}) async-start(bf16[512,8,512]{0,2,1:T(8,128)(2,1)} %bitcast.24), calls=%async_computation.2 | async-start | bytes 8388608 | tf_op jit(solution)/shard_map/all_to_all | solution.py:39
  244.0 653.8 %reduce-scatter.5.cloned.1.call-start = ((), (), s32[]{:S(2)}) async-start(), calls=%async_computation.5 | async-start | bytes 5242880 | tf_op jit(solution)/shard_map/reduce_scatter | solution.py:69
  508.3 392.4 %all-gather.8.cloned.1.call-start = ((), (), s32[]{:S(2)}) async-start(), calls=%async_computation.7 | async-start | bytes 7864320 | tf_op jit(solution)/shard_map/all_gather | solution.py:63
  508.4 21.3 %slice-start = ((s8[4718592]{0:T(1024)(128)(4,1)}), s8[524288]{0:T(1024)(128)(4,1)S(1)}, s32[]{:S(2)}) async-start(s8[4718592]{0:T(1024)(128)(4,1)} %bitcast.21), calls=%async_computation.8 | async-start | bytes 1048576
  518.2 11.5 %slice-start.1 = ((s8[4718592]{0:T(1024)(128)(4,1)}), s8[4194304]{0:T(1024)(128)(4,1)S(1)}, s32[]{:S(2)}) async-start(s8[4718592]{0:T(1024)(128)(4,1)} %bitcast.21), calls=%async_computation.9 | async-start | bytes 8388608
  518.2 219.4 %collective-permute-start = (bf16[4096,768]{1,0:T(8,128)(2,1)}, bf16[4096,768]{1,0:T(8,128)(2,1)}, u32[]{:S(2)}, u32[]{:S(2)}) collective-permute-start(bf16[4096,768]{1,0:T(8,128)(2,1)} %constant_dynamic-slice_fusion), channel_id=1, source_target_pairs={{0,1},{4,5},{9,10},{13,14},{18,19},{22,23},{27,24},{31,28}} | collective-permute-start | bytes 18874376 | tf_op jit(solution)/shard_map/ppermute | solution.py:26
  532.3 101.3 %collective-permute-start.2 = (bf16[768,1536]{1,0:T(8,128)(2,1)}, bf16[768,1536]{1,0:T(8,128)(2,1)S(1)}, u32[]{:S(2)}, u32[]{:S(2)}) collective-permute-start(bf16[768,1536]{1,0:T(8,128)(2,1)} %get-tuple-element.4), channel_id=1, source_target_pairs={{0,4},{4,8},{8,12},{12,16},{16,20},{20,24},{24,28},{28,0},{1,5},{5... | collective-permute-start | bytes 7077896 | tf_op jit(solution)/shard_map/ppermute | solution.py:49
  552.1 83.9 %collective-permute-start.3 = (bf16[768,1536]{1,0:T(8,128)(2,1)}, bf16[768,1536]{1,0:T(8,128)(2,1)}, u32[]{:S(2)}, u32[]{:S(2)}) collective-permute-start(bf16[768,1536]{1,0:T(8,128)(2,1)} %get-tuple-element.4), channel_id=1, source_target_pairs={{0,28},{4,0},{8,4},{12,8},{16,12},{20,16},{24,20},{28,24},{1,29},{... | collective-permute-start | bytes 7077896 | tf_op jit(solution)/shard_map/ppermute | solution.py:54
  633.6 101.5 %collective-permute-start.4 = (bf16[768,1536]{1,0:T(8,128)(2,1)S(1)}, bf16[768,1536]{1,0:T(8,128)(2,1)}, u32[]{:S(2)}, u32[]{:S(2)}) collective-permute-start(bf16[768,1536]{1,0:T(8,128)(2,1)S(1)} %collective-permute-done.2), channel_id=1, source_target_pairs={{0,4},{4,8},{8,12},{12,16},{16,20},{20,24},{24,28},{28,0},{1,5},{5... | collective-permute-start | bytes 7077896 | tf_op jit(solution)/shard_map/ppermute | solution.py:49
  636.0 119.9 %collective-permute-start.5 = (bf16[768,1536]{1,0:T(8,128)(2,1)}, bf16[768,1536]{1,0:T(8,128)(2,1)}, u32[]{:S(2)}, u32[]{:S(2)}) collective-permute-start(bf16[768,1536]{1,0:T(8,128)(2,1)} %collective-permute-done.3), channel_id=1, source_target_pairs={{0,28},{4,0},{8,4},{12,8},{16,12},{20,16},{24,20},{28,24},{1,29},{... | collective-permute-start | bytes 7077896 | tf_op jit(solution)/shard_map/ppermute | solution.py:54
  735.1 102.1 %collective-permute-start.6 = (bf16[768,1536]{1,0:T(8,128)(2,1)}, bf16[768,1536]{1,0:T(8,128)(2,1)}, u32[]{:S(2)}, u32[]{:S(2)}) collective-permute-start(bf16[768,1536]{1,0:T(8,128)(2,1)} %collective-permute-done.4), channel_id=1, source_target_pairs={{0,4},{4,8},{8,12},{12,16},{16,20},{20,24},{24,28},{28,0},{1,5},{5... | collective-permute-start | bytes 7077896 | tf_op jit(solution)/shard_map/ppermute | solution.py:49
  747.8 170.0 %collective-permute-start.1 = (bf16[4096,768]{1,0:T(8,128)(2,1)}, bf16[4096,768]{1,0:T(8,128)(2,1)}, u32[]{:S(2)}, u32[]{:S(2)}) collective-permute-start(bf16[4096,768]{1,0:T(8,128)(2,1)} %broadcast_select_fusion), channel_id=1, source_target_pairs={{0,2},{1,3},{4,6},{5,7},{9,11},{10,8},{13,15},{14,12},{18,16},{19,... | collective-permute-start | bytes 18874376 | tf_op jit(solution)/shard_map/ppermute | solution.py:26
  755.9 98.5 %collective-permute-start.7 = (bf16[768,1536]{1,0:T(8,128)(2,1)}, bf16[768,1536]{1,0:T(8,128)(2,1)}, u32[]{:S(2)}, u32[]{:S(2)}) collective-permute-start(bf16[768,1536]{1,0:T(8,128)(2,1)} %collective-permute-done.5), channel_id=1, source_target_pairs={{0,28},{4,0},{8,4},{12,8},{16,12},{20,16},{24,20},{28,24},{1,29},{... | collective-permute-start | bytes 7077896 | tf_op jit(solution)/shard_map/ppermute | solution.py:54
  837.1 57.4 %collective-permute-start.8 = (bf16[768,1536]{1,0:T(8,128)(2,1)}, bf16[768,1536]{1,0:T(8,128)(2,1)}, u32[]{:S(2)}, u32[]{:S(2)}) collective-permute-start(bf16[768,1536]{1,0:T(8,128)(2,1)} %collective-permute-done.6), channel_id=1, source_target_pairs={{0,4},{4,8},{8,12},{12,16},{16,20},{20,24},{24,28},{28,0},{1,5},{5... | collective-permute-start | bytes 7077896 | tf_op jit(solution)/shard_map/ppermute | solution.py:49
  851.0 46.8 %copy-start.3 = (f32[512,1024]{1,0:T(8,128)S(1)}, f32[512,1024]{1,0:T(8,128)}, u32[]{:S(2)}) copy-start(f32[512,1024]{1,0:T(8,128)} %param.8) | copy-start | bytes 6291460
  917.8 18.2 %copy-start.1 = (bf16[1024,1536]{1,0:T(8,128)(2,1)S(1)}, bf16[1024,1536]{1,0:T(8,128)(2,1)}, u32[]{:S(2)}) copy-start(bf16[1024,1536]{1,0:T(8,128)(2,1)} %param.7) | copy-start | bytes 9437188
Sparse Core Ops, SparseCore 0:
  29.2 209.9 reduce-scatter.2
Sparse Core Ops, SparseCore 1:
  32.1 37.0 all-gather.5
  239.3 250.7 all-gather.3
  508.4 43.2 reduce-scatter.4
  553.4 57.5 all-gather.7
